TPU v7x, 256 devices: a whole 4x4x8 slice. The times are simulated.
256 devices in a mesh: energy: 64 (over z, x, core), mom: 4 (over y).
Axes of the slice: x: 4, y: 4, z: 8, core: 2. Of those that a mesh axis runs over, the one named last changes fastest.
Arguments:
- green_less: float32 [4, 64, 64, 64, 128], P('mom', 'energy'), may hold values from -6 to 6
- couplings: bfloat16 [32, 3, 64, 64], replicated, may hold values from -0.75 to 0.75
- pair_atoms: int32 [64, 2], replicated, may hold values from 0 to 31
- shift_idx: int32 [3], replicated, may hold values from 1 to 4, as said below
- weights: float32 [2, 3, 4], replicated, may hold values from 0.05 to 1
Outputs:
- sigma_less: float32 [4, 64, 64, 64, 128], P('mom', 'energy')
Inputs may be any that keep to these rules, and one draw needn't show every extreme that they name: `shift_idx`: one mode's shift is exactly 4 and another's is exactly 1.
All inputs are finite; a program needn't handle non-finite values.
Results may differ from a plain program's by a relative error of at most 0.0003.
Values sent between devices are 32-bit elements; how exact they have to be, the bound alone decides.
No kernel may reach another device: no remote copies, remote signals or barrier semaphores. Data moves between devices by JAX's collectives and lax.ppermute only.
A program may use at most 64 MiB of HBM per device.

v0:
```python
import jax
import jax.numpy as jnp
from jax import lax
from jax.sharding import PartitionSpec as P

NMODE = 3


precise = lax.Precision.HIGHEST


def mixing_block(weights, target_ids, source_ids):
    moments = weights.shape[2]
    offset = (target_ids[:, None] - source_ids[None, :]) % moments
    selector = (offset[:, :, None] == jnp.arange(moments, dtype=jnp.int32)[None, None, :]).astype(
        jnp.float32
    )
    return jnp.einsum("slm,tjm->sltj", weights, selector, precision=precise)


def energy_operator(weights, shift_idx, target_ids, source_ids, energies):
    mixing = mixing_block(weights, target_ids, source_ids)
    energy_ids = jnp.arange(energies, dtype=jnp.int32)
    distance = energy_ids[None, :, None] - energy_ids[None, None, :]
    shifts = shift_idx[:, None, None]
    below_mask = (distance == shifts).astype(jnp.float32)
    above_mask = (distance == -shifts).astype(jnp.float32)
    below_part = mixing[0][:, :, None, :, None] * below_mask[:, None, :, None, :]
    above_part = mixing[1][:, :, None, :, None] * above_mask[:, None, :, None, :]
    return below_part + above_part


def apply_operator(operator, green_piece):
    sources = green_piece.shape[0]
    energies = green_piece.shape[1]
    flat = green_piece.reshape(sources, energies, -1)
    return jnp.einsum("ltejf,jfx->ltex", operator, flat, precision=precise)


def contract(mixed_flat, left_table, right_blocks, pair_dev, orbitals):
    mode_count = mixed_flat.shape[0]
    targets = mixed_flat.shape[1]
    energies = mixed_flat.shape[2]
    mixed = mixed_flat.reshape(mode_count, targets, energies, pair_dev, orbitals, 2 * orbitals)
    right_product = jnp.einsum("ltepac,lpcd->ltepad", mixed, right_blocks, precision=precise)
    return jnp.einsum("lpab,ltepbd->tepad", left_table, right_product, precision=precise)


def pair_couplings(couplings, atom_ids):
    atom_count = couplings.shape[0]
    orbitals = couplings.shape[2]
    onehot = (atom_ids[:, None] == jnp.arange(atom_count, dtype=jnp.int32)[None, :]).astype(
        jnp.bfloat16
    )
    selected = jnp.dot(
        onehot, couplings.reshape(atom_count, -1), preferred_element_type=jnp.float32
    )
    return selected.reshape(atom_ids.shape[0], NMODE, orbitals, orbitals).transpose(1, 0, 2, 3)


def block_diagonal(right_table):
    orbitals = right_table.shape[2]
    identity = jnp.eye(2, dtype=jnp.float32)
    blocks = jnp.einsum("qr,lpdc->lpqcrd", identity, right_table, precision=precise)
    return blocks.reshape(right_table.shape[0], right_table.shape[1], 2 * orbitals, 2 * orbitals)


def on_device(green_less, couplings, pair_atoms, shift_idx, weights):
    relaid = lax.all_to_all(green_less, "energy", split_axis=2, concat_axis=1, tiled=True)
    mom_dev = relaid.shape[0]
    energies = relaid.shape[1]
    pair_dev = relaid.shape[2]
    orbitals = relaid.shape[3]
    pair_start = lax.axis_index("energy") * pair_dev
    local_atoms = lax.dynamic_slice_in_dim(pair_atoms, pair_start, pair_dev, 0)
    left_table = pair_couplings(couplings, local_atoms[:, 0])
    right_blocks = block_diagonal(pair_couplings(couplings, local_atoms[:, 1]))
    own_moms = lax.axis_index("mom") * mom_dev + jnp.arange(mom_dev, dtype=jnp.int32)
    shard_piece = lax.all_gather(relaid, "mom", axis=0, tiled=True)
    source_ids = jnp.arange(shard_piece.shape[0], dtype=jnp.int32)
    operator = energy_operator(weights, shift_idx, own_moms, source_ids, energies)
    mixed_all = apply_operator(operator, shard_piece)
    result = contract(mixed_all, left_table, right_blocks, pair_dev, orbitals)
    return lax.all_to_all(result, "energy", split_axis=1, concat_axis=2, tiled=True)


def solution(mesh):
    return jax.shard_map(
        on_device,
        mesh=mesh,
        in_specs=(P("mom", "energy", None, None, None), P(), P(), P(), P()),
        out_specs=P("mom", "energy", None, None, None),
        check_vma=False,
    )
```

profile of v0, /device:TPU:96, one launch (start us, length us, event | category | flops | bytes accessed | tf_op | source)
XLA Modules:
  0.0 253.0 jit_solution(987305096567158454)
XLA Ops:
  6.5 0.0 copy-start
  6.5 0.0 copy-start.3
  6.5 0.0 copy-start.1
  6.5 0.0 copy-start.2
  6.5 0.0 all-gather.3.cloned.1.call-start
  6.6 60.4 %all_to_all.24 = f32[1,1,64,64,128]{4,3,1,0,2:T(8,128)} all-to-all(f32[1,1,64,64,128]{4,3,1,0,2:T(8,128)} %bitcast.94), channel_id=1, replica_groups=mesh['energy'=64,'mom'=4] {'energy'}, dimensions={2} | all-to-all | bytes 4194304 | tf_op jit(solution)/shard_map/all_to_all | solution.py:69
  67.0 0.0 all-gather.3.cloned.1.call-update
  67.0 0.0 copy-done.3
  67.0 0.0 copy-done.1
  67.0 1.3 reshape.178
  68.4 1.7 reshape.179
  70.1 0.0 copy-done.2
  70.1 0.1 constant_dynamic-slice_fusion
  70.2 0.5 fusion.36
  70.7 1.6 fusion.12
  72.3 0.1 copy.26
  72.4 0.2 multiply_bitcast_fusion
  72.6 0.2 reshape.192
  72.9 0.0 copy-done
  72.9 0.2 convolution_bitcast_fusion
  73.1 0.1 compare_convert_fusion.1
  73.2 1.5 fusion.10
  74.7 76.5 %all-gather.3.cloned.1.call-done = f32[4,1,64,64,128]{4,3,2,1,0:T(8,128)} async-done(((f32[1,1,64,64,128]{4,3,2,1,0:T(8,128)}), f32[4,1,64,64,128]{4,3,2,1,0:T(8,128)}) %all-gather.3.cloned.1.call-update) | async-done | bytes 8388624 | tf_op jit(solution)/shard_map/all_gather | solution.py:79
  151.2 9.4 %reshape.181 = f32[4,64,8192]{2,1,0:T(8,128)} reshape(f32[4,1,64,64,128]{4,3,2,1,0:T(8,128)} %all-gather.3.cloned.1.call-done) | data formatting | bytes 16777216 | tf_op jit(solution)/shard_map/reshape | solution.py:36
  160.6 8.7 %fusion.6 = f32[3,64,64,128]{3,1,2,0:T(8,128)S(1)} fusion(f32[3,64,64]{2,1,0:T(8,128)S(1)} %get-tuple-element.6, f32[3,4]{1,0:T(4,128)S(1)} %get-tuple-element.8, f32[3,64,64]{2,1,0:T(8,128)S(1)} %get-tuple-element.5, f32[3,4]{1,0:T(4,128)S(1)} %get-tuple-element.7, f32[4,64,8192]{2,1,0:T(8,128)} %reshape.181), kind=kOutput, calls=%fused_computation.7 | convolution fusion | flops 4831985664 | bytes 14778464 | tf_op jit(solution)/shard_map/ltejf,jfx->ltex/dot_general | solution.py:37
  169.3 11.5 %fusion.4 = f32[3,128,64,64]{1,3,2,0:T(8,128)S(1)} fusion(f32[3,64,64,128]{3,1,2,0:T(8,128)S(1)} %fusion.6, f32[3,128,128,1]{2,1,0,3:T(8,128)S(1)} %reshape.192), kind=kOutput, calls=%fused_computation.5 | convolution fusion | flops 2415919104 | bytes 12779520 | tf_op jit(solution)/shard_map/ltepac,lpcd->ltepad/dot_general | solution.py:45
  180.8 4.5 %fusion.7 = f32[1,64,1,64,128]{4,3,0,2,1:T(8,128)S(1)} fusion(f32[3,64,64,1]{2,1,3,0:T(8,128)S(1)} %bitcast.95, f32[3,128,64,64]{1,3,2,0:T(8,128)S(1)} %fusion.4), kind=kOutput, calls=%fused_computation.8 | convolution fusion | flops 1207959552 | bytes 8437760 | tf_op jit(solution)/shard_map/lpab,ltepbd->tepad/dot_general | solution.py:46
  185.4 59.5 %all_to_all.25 = f32[1,64,1,64,128]{4,3,0,2,1:T(8,128)S(1)} all-to-all(f32[1,64,1,64,128]{4,3,0,2,1:T(8,128)S(1)} %fusion.7), channel_id=1, replica_groups=mesh['energy'=64,'mom'=4] {'energy'}, dimensions={1} | all-to-all | bytes 4194304 | tf_op jit(solution)/shard_map/all_to_all | solution.py:84
  244.9 1.3 copy.49
  (5 shorter events, 0.0 us)
Async XLA Ops:
  6.5 66.3 %copy-start = (f32[2,3,4]{2,0,1:T(2,128)S(1)}, f32[2,3,4]{2,0,1:T(2,128)}, u32[]{:S(2)}) copy-start(f32[2,3,4]{2,0,1:T(2,128)} %param.9) | copy-start | bytes 292
  6.5 60.5 %copy-start.3 = (s32[3]{0:T(128)S(1)}, s32[3]{0:T(128)}, u32[]{:S(2)}) copy-start(s32[3]{0:T(128)} %param.8) | copy-start | bytes 40
  6.5 60.5 %copy-start.1 = (bf16[32,3,64,64]{3,2,1,0:T(8,128)(2,1)S(1)}, bf16[32,3,64,64]{3,2,1,0:T(8,128)(2,1)}, u32[]{:S(2)}) copy-start(bf16[32,3,64,64]{3,2,1,0:T(8,128)(2,1)} %param.6) | copy-start | bytes 2359300
  6.5 63.6 %copy-start.2 = (s32[64,2]{0,1:T(2,128)S(1)}, s32[64,2]{0,1:T(2,128)}, u32[]{:S(2)}) copy-start(s32[64,2]{0,1:T(2,128)} %param.7) | copy-start | bytes 1540
  6.5 144.7 %all-gather.3.cloned.1.call-start = ((), (), s32[]{:S(2)}) async-start(), calls=%async_computation.2 | async-start | bytes 10485760 | tf_op jit(solution)/shard_map/all_gather | solution.py:79
Sparse Core Ops, SparseCore 0:
  67.1 84.0 all-gather.2
where the time goes:
time: 257 us; the launch traced here: 253 us
  blocking collectives  120 us (47%)
  waiting for transfers between devices  76.5 us (30%)
  matrix products  28.1 us (11%)
  local copies, waits for them, and re-layouts  14.7 us (6%)
  between operations  13.5 us (5%)
    all_gather x1, waiting for transfers between devices, on_device(): shard_piece = lax.all_gather(relaid, 'mom', axis=0, tiled=True)  76.5 us
    all_to_all x1, blocking collectives, on_device(): lax.all_to_all(green_less, 'energy', split_axis=2, concat_axis=1, tiled=T...  60.4 us
    all_to_all x1, blocking collectives, on_device(): lax.all_to_all(result, 'energy', split_axis=1, concat_axis=2, tiled=True)  59.5 us
    dot_general x1, matrix products, contract(): jnp.einsum('ltepac,lpcd->ltepad', mixed, right_blocks, precision=precise)  11.5 us
    reshape x1, local copies, waits for them, and re-layouts, apply_operator(): flat = green_piece.reshape(sources, energies, -1)  9.36 us
    dot_general x1, matrix products, apply_operator(): return jnp.einsum('ltejf,jfx->ltex', operator, flat, precision=precise)  8.71 us
  transfers between devices with their start and end apart: 1, of which 1 were waited for; matrix products, arithmetic and copies ran while one was open for 3% of the time, Pallas kernels for 0%

commit v1 on v0

v1 whole, which is shorter than its diff:
```python
import functools

import jax
import jax.numpy as jnp
from jax import lax
from jax.experimental import pallas as pl
from jax.experimental.pallas import tpu as pltpu
from jax.sharding import Mesh
from jax.sharding import PartitionSpec as P

NMODE = 3
HALO = 4
VMEM_BYTES = 16 * 2**20
LIMIT = pltpu.CompilerParams(vmem_limit_bytes=VMEM_BYTES)
GROUP = ("x", "c", "y")


def tables_kernel(atoms, coupling_hbm, left_ref, right_ref, picked, sems):
    pairs = left_ref.shape[0]
    copies = []
    for pair in range(pairs):
        for side in range(2):
            copy = pltpu.make_async_copy(
                coupling_hbm.at[atoms[pair, side]], picked.at[pair, side], sems.at[pair, side]
            )
            copy.start()
            copies.append(copy)
    for copy in copies:
        copy.wait()
    size = picked.shape[-1]
    nothing = jnp.zeros((size, size), jnp.float32)
    for pair in range(pairs):
        lefts = []
        for mode in range(NMODE):
            left = picked[pair, 0, mode].astype(jnp.float32)
            lefts += [left, left]
            turned = picked[pair, 1, mode].astype(jnp.float32).T
            upper = jnp.concatenate([turned, nothing], axis=1)
            lower = jnp.concatenate([nothing, turned], axis=1)
            both = jnp.concatenate([upper, lower], axis=0).astype(jnp.bfloat16)
            right_ref[pair, mode, 0] = both
            right_ref[pair, mode, 1] = both
        left_ref[pair] = jnp.concatenate(lefts, axis=1).astype(jnp.bfloat16)


def tables(atoms, couplings):
    pairs, size = atoms.shape[0], couplings.shape[-1]
    return pl.pallas_call(
        tables_kernel,
        grid_spec=pltpu.PrefetchScalarGridSpec(
            num_scalar_prefetch=1,
            grid=(1,),
            in_specs=[pl.BlockSpec(memory_space=pl.ANY)],
            out_specs=[
                pl.BlockSpec((pairs, size, 2 * NMODE * size), lambda i, a: (0, 0, 0)),
                pl.BlockSpec((pairs, NMODE, 2, 2 * size, 2 * size), lambda i, a: (0, 0, 0, 0, 0)),
            ],
            scratch_shapes=[
                pltpu.VMEM((pairs, 2, NMODE, size, size), jnp.bfloat16),
                pltpu.SemaphoreType.DMA((pairs, 2)),
            ],
        ),
        out_shape=[
            jax.ShapeDtypeStruct((pairs, size, 2 * NMODE * size), jnp.bfloat16),
            jax.ShapeDtypeStruct((pairs, NMODE, 2, 2 * size, 2 * size), jnp.bfloat16),
        ],
        compiler_params=LIMIT,
        cost_estimate=pl.CostEstimate(flops=1000000, bytes_accessed=4000000, transcendentals=0),
        name="tables",
    )(atoms, couplings)


def fold_kernel(block_ref, low_ref, high_ref):
    half = low_ref.shape[0]
    for energy in range(2 * half):
        target = low_ref if energy < half else high_ref
        first, second, third, fourth = (block_ref[energy, moment] for moment in range(4))
        even, odd = first + third, second + fourth
        target[energy % half, 0] = even + odd
        target[energy % half, 1] = even - odd
        target[energy % half, 2] = first - third
        target[energy % half, 3] = second - fourth


def fold(block, pair):
    energies, moments, _, rows, columns = block.shape
    half = (energies // 2, moments, rows, columns)
    vmem = pl.BlockSpec(half, lambda i: (0, 0, 0, 0))
    return pl.pallas_call(
        fold_kernel,
        grid=(1,),
        in_specs=[
            pl.BlockSpec((energies, moments, None, rows, columns), lambda i: (0, 0, pair, 0, 0))
        ],
        out_specs=[vmem, vmem],
        out_shape=[jax.ShapeDtypeStruct(half, jnp.float32)] * 2,
        compiler_params=LIMIT,
        cost_estimate=pl.CostEstimate(flops=1000000, bytes_accessed=4000000, transcendentals=0),
        name="fold",
    )(block)


def mix_kernel(shifts, weights, below, low, high, above, left_ref, right_ref, *rest):
    out_ref, window, sems = rest[-3:]
    quarter = low.shape[0]
    copies = [
        pltpu.make_async_copy(part, window.at[pl.ds(place * quarter, quarter)], sems.at[place])
        for place, part in enumerate((below, low, high, above))
    ]
    for copy in copies:
        copy.start()
    factors = []
    for mode in range(NMODE):
        for side in range(2):
            w0, w1, w2, w3 = (weights[side, mode, moment] for moment in range(4))
            even, odd = w0 + w2, w1 + w3
            factors.append(
                ((even + odd) * 0.25, (even - odd) * 0.25, (w0 - w2) * 0.5, (w1 - w3) * 0.5)
            )
    for copy in copies:
        copy.wait()
    rows = window.shape[2]

    def one_energy(energy, carry):
        stacked = [[] for _ in range(4)]
        for mode in range(NMODE):
            shift = shifts[mode]
            parts = []
            for side, place in ((0, energy + HALO - shift), (1, energy + HALO + shift)):
                p, q, r, s = factors[2 * mode + side]
                total, swing, d0, d1 = (window[place, part] for part in range(4))
                parts.append((p * total, q * swing, r * d0 - s * d1, s * d0 + r * d1))
            mixed = jnp.concatenate([a + b for a, b in zip(*parts)], axis=0)
            coarse = mixed.astype(jnp.bfloat16)
            fine = (mixed - coarse.astype(jnp.float32)).astype(jnp.bfloat16)
            right = right_ref[mode].reshape(2 * right_ref.shape[2], right_ref.shape[3])
            product = jnp.dot(
                jnp.concatenate([coarse, fine], axis=1), right, preferred_element_type=jnp.float32
            )
            coarse = product.astype(jnp.bfloat16)
            fine = (product - coarse.astype(jnp.float32)).astype(jnp.bfloat16)
            for part in range(4):
                block = slice(part * rows, (part + 1) * rows)
                stacked[part] += [coarse[block], fine[block]]
        columns = jnp.concatenate([jnp.concatenate(pieces, axis=0) for pieces in stacked], axis=1)
        total = jnp.dot(left_ref[...], columns, preferred_element_type=jnp.float32)
        width = out_ref.shape[3]
        plain, swing, v0, v1 = (total[:, part * width : (part + 1) * width] for part in range(4))
        even, odd = plain + swing, plain - swing
        out_ref[energy, 0] = even + v0
        out_ref[energy, 1] = odd + v1
        out_ref[energy, 2] = even - v0
        out_ref[energy, 3] = odd - v1
        return carry

    lax.fori_loop(0, out_ref.shape[0], one_energy, 0, unroll=4)


def mix(shifts, weights, below, low, high, above, left, right, pair, pairs, into=None):
    quarter, moments, rows, columns = low.shape
    shape = (2 * quarter, moments, pairs, rows, columns)
    hbm = pl.BlockSpec(memory_space=pl.ANY)
    smem = pl.BlockSpec(memory_space=pltpu.SMEM)
    held = [] if into is None else [into]
    return pl.pallas_call(
        mix_kernel,
        grid=(1,),
        in_specs=[
            smem,
            smem,
            hbm,
            hbm,
            hbm,
            hbm,
            pl.BlockSpec((None, *left.shape[1:]), lambda i: (pair, 0, 0)),
            pl.BlockSpec((None, *right.shape[1:]), lambda i: (pair, 0, 0, 0, 0)),
            *(hbm for _ in held),
        ],
        out_specs=pl.BlockSpec(
            (2 * quarter, moments, None, rows, columns), lambda i: (0, 0, pair, 0, 0)
        ),
        out_shape=jax.ShapeDtypeStruct(shape, jnp.float32),
        scratch_shapes=[
            pltpu.VMEM((4 * quarter, *low.shape[1:]), jnp.float32),
            pltpu.SemaphoreType.DMA((4,)),
        ],
        input_output_aliases={8: 0} if held else {},
        compiler_params=LIMIT,
        cost_estimate=pl.CostEstimate(flops=5000000000, bytes_accessed=4000000, transcendentals=0),
        name="mix",
    )(shifts, weights, below, low, high, above, left, right, *held)


def on_device(green_less, couplings, pair_atoms, shift_idx, weights):
    pairs, rows, columns = green_less.shape[2:]
    group = lax.axis_size(GROUP)
    moments = lax.axis_size("y")
    planes = lax.axis_size("z")
    here = lax.axis_index(GROUP)
    up = [(plane, plane + 1) for plane in range(planes - 1)]
    down = [(plane + 1, plane) for plane in range(planes - 1)]
    owned = pairs // group
    atoms = lax.dynamic_slice_in_dim(pair_atoms, here * owned, owned, 0)
    left, right = tables(atoms, couplings)
    moved = lax.all_to_all(
        green_less.reshape(group, owned, rows, columns), GROUP, 0, 0, tiled=True
    )
    block = moved.reshape(group // moments, moments, owned, rows, columns)
    halves = []
    for pair in range(owned):
        low, high = fold(block, pair)
        halves.append((lax.ppermute(high, "z", up), low, high, lax.ppermute(low, "z", down)))
    result = None
    for pair in range(owned):
        result = mix(shift_idx, weights, *halves[pair], left, right, pair, owned, result)
    back = lax.all_to_all(
        result.reshape(group, owned, rows, columns), GROUP, 0, 0, tiled=True
    )
    return back.reshape(green_less.shape)


def solution(mesh):
    sizes = dict(mesh.shape)
    chips = sizes["energy"] // 8
    split = Mesh(
        mesh.devices.reshape(chips, 4, 2, sizes["mom"]), ("z", "x", "c", "y")
    )
    placed = P("y", ("z", "x", "c"), None, None, None)

    def step(*args):
        return jax.shard_map(
            on_device,
            mesh=split,
            in_specs=(placed, P(), P(), P(), P()),
            out_specs=placed,
            check_vma=False,
        )(*args)

    return step
```

time: 257 us -> 107 us (0.42); the launches traced: 253 us -> 106 us
  waiting for transfers between devices: 76.5 us -> 10.3 us
  blocking collectives: 120 us -> 68 us
  matrix products: 28.1 us -> 0 us
  starting transfers between devices: 0.03 us -> 14 us
  between operations: 13.5 us -> 0.11 us
  local copies, waits for them, and re-layouts: 14.7 us -> 2.92 us
  Pallas kernels: 0 us -> 10.9 us
    all_gather x1 -> x0, waiting for transfers between devices: 76.5 us -> none  [on_device(): shard_piece = lax.all_gather(relaid, 'mom', axis=0, tiled=True)]
    all_to_all x2, blocking collectives: 120 us -> 68 us  [the longest x1 35.7 us: on_device(): lax.all_to_all(green_less.reshape(group, owned, rows, columns), GROUP, 0,...]
    dot_general x6 -> x0, matrix products: 28.1 us -> none  [the longest x1 11.5 us: contract(): jnp.einsum('ltepac,lpcd->ltepad', mixed, right_blocks, precision=precise)]
    ppermute x0 -> x4, starting transfers between devices: none -> 14 us  [the longest x2 10.2 us: on_device(): lax.ppermute(high, 'z', up)]
    pallas_call x0 -> x5, Pallas kernels: none -> 10.9 us  [the longest x2 8.67 us: mix(): pl.pallas_call(mix_kernel, grid=(1,), in_specs=[smem, smem, hbm, hbm, hbm...]
    reshape x2 -> x0, local copies, waits for them, and re-layouts: 10.7 us -> none  [the longest x1 9.36 us: apply_operator(): flat = green_piece.reshape(sources, energies, -1)]
    ppermute x0 -> x4, waiting for transfers between devices: none -> 10.3 us  [the longest x2 10.3 us: on_device(): lax.ppermute(low, 'z', down)]
  transfers between devices with their start and end apart: 1 -> 4, of which waited for: 1 -> 2; matrix products, arithmetic and copies ran while one was open for 3% -> 0% of each run, Pallas kernels for 0% -> 6%
where the time goes in v1:
time: 107 us; the launch traced here: 106 us
  blocking collectives  68 us (64%)
  starting transfers between devices  14 us (13%)
  Pallas kernels  10.9 us (10%)
  waiting for transfers between devices  10.3 us (10%)
  local copies, waits for them, and re-layouts  2.92 us (3%)
    all_to_all x1, blocking collectives, on_device(): lax.all_to_all(green_less.reshape(group, owned, rows, columns), GROUP, 0,...  35.7 us
    all_to_all x1, blocking collectives, on_device(): lax.all_to_all(result.reshape(group, owned, rows, columns), GROUP, 0, 0,...  32.3 us
    ppermute x2, waiting for transfers between devices, on_device(): lax.ppermute(low, 'z', down)  10.3 us
    ppermute x2, starting transfers between devices, on_device(): lax.ppermute(high, 'z', up)  10.2 us
    pallas_call x2, Pallas kernels, mix(): pl.pallas_call(mix_kernel, grid=(1,), in_specs=[smem, smem, hbm, hbm, hbm...  8.67 us
    ppermute x2, starting transfers between devices, on_device(): lax.ppermute(low, 'z', down)  3.84 us
    unnamed x11, local copies, waits for them, and re-layouts  2.84 us
  transfers between devices with their start and end apart: 4, of which 2 were waited for; matrix products, arithmetic and copies ran while one was open for 0% of the time, Pallas kernels for 6%

profile of v1, /device:TPU:96, one launch (start us, length us, event | category | flops | bytes accessed | tf_op | source)
XLA Modules:
  0.0 106.2 jit_solution(15282829934443987176)
XLA Ops:
  0.0 0.0 copy-start
  0.0 35.7 %all_to_all.10 = f32[32,2,64,128]{3,2,1,0:T(8,128)S(1)} all-to-all(f32[32,2,64,128]{3,2,1,0:T(8,128)} %bitcast.8), channel_id=1, replica_groups=mesh['z'=8,'x'=4,'c'=2,'y'=4] {'x','c','y'}, dimensions={0} | all-to-all | bytes 4194304 | tf_op jit(solution)/shard_map/all_to_all | solution.py:205
  35.7 0.0 copy-start.3
  35.7 0.1 fold.3
  35.8 0.0 copy-start.2
  35.8 5.0 %collective-permute-start.2 = (f32[4,4,64,128]{3,2,1,0:T(8,128)S(1)}, f32[4,4,64,128]{3,2,1,0:T(8,128)}, u32[]{:S(2)}, u32[]{:S(2)}) collective-permute-start(f32[4,4,64,128]{3,2,1,0:T(8,128)S(1)} %get-tuple-element.15.high), channel_id=1, source_target_pairs={{0,32},{32,64},{64,96},{96,128},{128,160},{160,192},{192,224},{1,3... | collective-permute-start | bytes 1572872 | tf_op jit(solution)/shard_map/ppermute | solution.py:212
  40.9 1.9 %collective-permute-start.3 = (f32[4,4,64,128]{3,2,1,0:T(8,128)S(1)}, f32[4,4,64,128]{3,2,1,0:T(8,128)}, u32[]{:S(2)}, u32[]{:S(2)}) collective-permute-start(f32[4,4,64,128]{3,2,1,0:T(8,128)S(1)} %get-tuple-element.16.low), channel_id=1, source_target_pairs={{32,0},{64,32},{96,64},{128,96},{160,128},{192,160},{224,192},{33,... | collective-permute-start | bytes 1572872 | tf_op jit(solution)/shard_map/ppermute | solution.py:212
  42.8 1.0 fold.2
  43.8 5.1 %collective-permute-start = (f32[4,4,64,128]{3,2,1,0:T(8,128)}, f32[4,4,64,128]{3,2,1,0:T(8,128)S(1)}, u32[]{:S(2)}, u32[]{:S(2)}) collective-permute-start(f32[4,4,64,128]{3,2,1,0:T(8,128)} %get-tuple-element.11.high), channel_id=1, source_target_pairs={{0,32},{32,64},{64,96},{96,128},{128,160},{160,192},{192,224},{1,3... | collective-permute-start | bytes 1572872 | tf_op jit(solution)/shard_map/ppermute | solution.py:212
  49.0 1.9 %collective-permute-start.1 = (f32[4,4,64,128]{3,2,1,0:T(8,128)}, f32[4,4,64,128]{3,2,1,0:T(8,128)S(1)}, u32[]{:S(2)}, u32[]{:S(2)}) collective-permute-start(f32[4,4,64,128]{3,2,1,0:T(8,128)} %get-tuple-element.12.low), channel_id=1, source_target_pairs={{32,0},{64,32},{96,64},{128,96},{160,128},{192,160},{224,192},{33,... | collective-permute-start | bytes 1572872 | tf_op jit(solution)/shard_map/ppermute | solution.py:212
  50.9 0.0 copy-done
  50.9 0.1 constant_dynamic-slice_fusion
  51.0 0.1 copy.10.atoms
  51.1 0.0 copy-done.3
  51.1 0.0 copy-start.1
  51.1 1.4 %copy-done.1 = bf16[32,3,64,64]{3,2,1,0:T(8,128)(2,1)S(1)} copy-done((bf16[32,3,64,64]{3,2,1,0:T(8,128)(2,1)S(1)}, bf16[32,3,64,64]{3,2,1,0:T(8,128)(2,1)}, u32[]{:S(2)}) %copy-start.1) | copy-done | bytes 786456
  52.5 1.1 %tables.1 = (bf16[2,64,384]{2,1,0:T(8,128)(2,1)S(1)}, bf16[2,3,2,128,128]{4,3,2,1,0:T(8,128)(2,1)S(1)}) custom-call(s32[2,2]{1,0:T(2,128)S(1)} %copy.10.atoms, bf16[32,3,64,64]{3,2,1,0:T(8,128)(2,1)S(1)} %copy-done.1), custom_call_target="tpu_custom_call" | custom-call | flops 1000000 | bytes 4000000 | tf_op jit(solution)/shard_map/tables/pallas_call | solution.py:48
  53.6 0.0 collective-permute-done.2.below
  53.6 5.3 %collective-permute-done.3.above = f32[4,4,64,128]{3,2,1,0:T(8,128)} collective-permute-done((f32[4,4,64,128]{3,2,1,0:T(8,128)S(1)}, f32[4,4,64,128]{3,2,1,0:T(8,128)}, u32[]{:S(2)}, u32[]{:S(2)}) %collective-permute-start.3) | collective-permute-done | bytes 524320 | tf_op jit(solution)/shard_map/ppermute | solution.py:212
  58.9 0.0 copy-done.2
  58.9 4.3 %mix.2.rest_0_ = f32[8,4,2,64,128]{4,3,2,1,0:T(8,128)S(1)} custom-call(s32[3]{0:T(128)S(1)} %copy-done.2, f32[2,3,4]{2,1,0:T(4,128)S(1)} %copy.9.weights, f32[4,4,64,128]{3,2,1,0:T(8,128)} %collective-permute-done.2.below, f32[4,4,64,128]{3,2,1,0:T(8,128)S(1)} %get-tuple-element.16.low, f32[4,4,64,128]{3,2,1,0:T(8,128)S(1)} %get-tuple-element.15.high, ...), custom_call_target="tpu_custom_call" | custom-call | flops 5000000000 | bytes 4000000 | tf_op jit(solution)/shard_map/mix/pallas_call | solution.py:165
  63.2 0.0 collective-permute-done.below
  63.2 5.0 %collective-permute-done.1.above = f32[4,4,64,128]{3,2,1,0:T(8,128)S(1)} collective-permute-done((f32[4,4,64,128]{3,2,1,0:T(8,128)}, f32[4,4,64,128]{3,2,1,0:T(8,128)S(1)}, u32[]{:S(2)}, u32[]{:S(2)}) %collective-permute-start.1) | collective-permute-done | bytes 524320 | tf_op jit(solution)/shard_map/ppermute | solution.py:212
  68.2 4.3 %mix.3 = f32[8,4,2,64,128]{4,3,2,1,0:T(8,128)S(1)} custom-call(s32[3]{0:T(128)S(1)} %copy-done.2, f32[2,3,4]{2,1,0:T(4,128)S(1)} %copy.9.weights, f32[4,4,64,128]{3,2,1,0:T(8,128)S(1)} %collective-permute-done.below, f32[4,4,64,128]{3,2,1,0:T(8,128)} %get-tuple-element.12.low, ...), custom_call_target="tpu_custom_call", output_to_operand_aliasing={{}: (8, {})} | custom-call | flops 5000000000 | bytes 4000000 | tf_op jit(solution)/shard_map/mix/pallas_call | solution.py:165
  72.6 32.3 %all_to_all.11 = f32[32,2,64,128]{3,2,1,0:T(8,128)S(1)} all-to-all(f32[32,2,64,128]{3,2,1,0:T(8,128)S(1)} %bitcast.6), channel_id=1, replica_groups=mesh['z'=8,'x'=4,'c'=2,'y'=4] {'x','c','y'}, dimensions={0} | all-to-all | bytes 4194304 | tf_op jit(solution)/shard_map/all_to_all | solution.py:216
  104.9 1.3 %copy.13 = f32[1,1,64,64,128]{4,3,2,1,0:T(8,128)} copy(f32[1,1,64,64,128]{4,3,2,1,0:T(8,128)S(1)} %bitcast.7) | data formatting | bytes 4194304
  (1 shorter events, 0.0 us)
Async XLA Ops:
  0.0 50.9 %copy-start = (s32[64,2]{0,1:T(2,128)S(1)}, s32[64,2]{0,1:T(2,128)}, u32[]{:S(2)}) copy-start(s32[64,2]{0,1:T(2,128)} %param.7) | copy-start | bytes 1540
  35.7 15.3 %copy-start.3 = (f32[2,3,4]{2,0,1:T(2,128)S(1)}, f32[2,3,4]{2,0,1:T(2,128)}, u32[]{:S(2)}) copy-start(f32[2,3,4]{2,0,1:T(2,128)} %param.9) | copy-start | bytes 292
  35.8 23.1 %copy-start.2 = (s32[3]{0:T(128)S(1)}, s32[3]{0:T(128)}, u32[]{:S(2)}) copy-start(s32[3]{0:T(128)} %shifts.3) | copy-start | bytes 40
  35.8 17.8 %collective-permute-start.2 = (f32[4,4,64,128]{3,2,1,0:T(8,128)S(1)}, f32[4,4,64,128]{3,2,1,0:T(8,128)}, u32[]{:S(2)}, u32[]{:S(2)}) collective-permute-start(f32[4,4,64,128]{3,2,1,0:T(8,128)S(1)} %get-tuple-element.15.high), channel_id=1, source_target_pairs={{0,32},{32,64},{64,96},{96,128},{128,160},{160,192},{192,224},{1,3... | collective-permute-start | bytes 1572872 | tf_op jit(solution)/shard_map/ppermute | solution.py:212
  40.9 18.0 %collective-permute-start.3 = (f32[4,4,64,128]{3,2,1,0:T(8,128)S(1)}, f32[4,4,64,128]{3,2,1,0:T(8,128)}, u32[]{:S(2)}, u32[]{:S(2)}) collective-permute-start(f32[4,4,64,128]{3,2,1,0:T(8,128)S(1)} %get-tuple-element.16.low), channel_id=1, source_target_pairs={{32,0},{64,32},{96,64},{128,96},{160,128},{192,160},{224,192},{33,... | collective-permute-start | bytes 1572872 | tf_op jit(solution)/shard_map/ppermute | solution.py:212
  43.8 19.4 %collective-permute-start = (f32[4,4,64,128]{3,2,1,0:T(8,128)}, f32[4,4,64,128]{3,2,1,0:T(8,128)S(1)}, u32[]{:S(2)}, u32[]{:S(2)}) collective-permute-start(f32[4,4,64,128]{3,2,1,0:T(8,128)} %get-tuple-element.11.high), channel_id=1, source_target_pairs={{0,32},{32,64},{64,96},{96,128},{128,160},{160,192},{192,224},{1,3... | collective-permute-start | bytes 1572872 | tf_op jit(solution)/shard_map/ppermute | solution.py:212
  49.0 19.3 %collective-permute-start.1 = (f32[4,4,64,128]{3,2,1,0:T(8,128)}, f32[4,4,64,128]{3,2,1,0:T(8,128)S(1)}, u32[]{:S(2)}, u32[]{:S(2)}) collective-permute-start(f32[4,4,64,128]{3,2,1,0:T(8,128)} %get-tuple-element.12.low), channel_id=1, source_target_pairs={{32,0},{64,32},{96,64},{128,96},{160,128},{192,160},{224,192},{33,... | collective-permute-start | bytes 1572872 | tf_op jit(solution)/shard_map/ppermute | solution.py:212
  51.1 1.4 %copy-start.1 = (bf16[32,3,64,64]{3,2,1,0:T(8,128)(2,1)S(1)}, bf16[32,3,64,64]{3,2,1,0:T(8,128)(2,1)}, u32[]{:S(2)}) copy-start(bf16[32,3,64,64]{3,2,1,0:T(8,128)(2,1)} %coupling_hbm.1) | copy-start | bytes 2359300

commit v2 on v1

--- a/solution.py
+++ b/solution.py
@@ -1,4 +1,5 @@
 import functools
+import itertools
 
 import jax
 import jax.numpy as jnp
@@ -9,10 +10,10 @@
 from jax.sharding import PartitionSpec as P
 
 NMODE = 3
-HALO = 4
 VMEM_BYTES = 16 * 2**20
 LIMIT = pltpu.CompilerParams(vmem_limit_bytes=VMEM_BYTES)
 GROUP = ("x", "c", "y")
+AXES = ("z", "x", "c", "y")
 
 
 def tables_kernel(atoms, coupling_hbm, left_ref, right_ref, picked, sems):
@@ -100,15 +101,15 @@
     )(block)
 
 
-def mix_kernel(shifts, weights, below, low, high, above, left_ref, right_ref, *rest):
-    out_ref, window, sems = rest[-3:]
-    quarter = low.shape[0]
-    copies = [
-        pltpu.make_async_copy(part, window.at[pl.ds(place * quarter, quarter)], sems.at[place])
-        for place, part in enumerate((below, low, high, above))
-    ]
-    for copy in copies:
-        copy.start()
+def mix_kernel(split, place, shifts, weights, first_ref, second_ref, third_ref, left_ref, right_ref, *rest):
+    if split:
+        kept_ref, away_ref, window, out_ref = rest[-4:]
+    else:
+        out_ref, window = rest[-2:]
+    quarter = first_ref.shape[0]
+    for spot, part in enumerate((first_ref, second_ref, third_ref)):
+        for energy in range(quarter):
+            window[spot * quarter + energy] = part[energy]
     factors = []
     for mode in range(NMODE):
         for side in range(2):
@@ -117,8 +118,6 @@
             factors.append(
                 ((even + odd) * 0.25, (even - odd) * 0.25, (w0 - w2) * 0.5, (w1 - w3) * 0.5)
             )
-    for copy in copies:
-        copy.wait()
     rows = window.shape[2]
 
     def one_energy(energy, carry):
@@ -126,9 +125,9 @@
         for mode in range(NMODE):
             shift = shifts[mode]
             parts = []
-            for side, place in ((0, energy + HALO - shift), (1, energy + HALO + shift)):
+            for side, spot in ((0, energy + quarter - shift), (1, energy + quarter + shift)):
                 p, q, r, s = factors[2 * mode + side]
-                total, swing, d0, d1 = (window[place, part] for part in range(4))
+                total, swing, d0, d1 = (window[spot, part] for part in range(4))
                 parts.append((p * total, q * swing, r * d0 - s * d1, s * d0 + r * d1))
             mixed = jnp.concatenate([a + b for a, b in zip(*parts)], axis=0)
             coarse = mixed.astype(jnp.bfloat16)
@@ -144,51 +143,168 @@
                 stacked[part] += [coarse[block], fine[block]]
         columns = jnp.concatenate([jnp.concatenate(pieces, axis=0) for pieces in stacked], axis=1)
         total = jnp.dot(left_ref[...], columns, preferred_element_type=jnp.float32)
-        width = out_ref.shape[3]
+        width = out_ref.shape[-1]
         plain, swing, v0, v1 = (total[:, part * width : (part + 1) * width] for part in range(4))
         even, odd = plain + swing, plain - swing
-        out_ref[energy, 0] = even + v0
-        out_ref[energy, 1] = odd + v1
-        out_ref[energy, 2] = even - v0
-        out_ref[energy, 3] = odd - v1
+        for moment, value in enumerate((even + v0, odd + v1, even - v0, odd - v1)):
+            if split:
+                away = jnp.where(lax.rem(energy, 2) == place[0], 0, 1)
+                out_ref[away, energy // 2, moment] = value
+            else:
+                out_ref[energy, moment] = value
         return carry
 
-    lax.fori_loop(0, out_ref.shape[0], one_energy, 0, unroll=4)
-
-
-def mix(shifts, weights, below, low, high, above, left, right, pair, pairs, into=None):
-    quarter, moments, rows, columns = low.shape
-    shape = (2 * quarter, moments, pairs, rows, columns)
-    hbm = pl.BlockSpec(memory_space=pl.ANY)
+    lax.fori_loop(0, quarter, one_energy, 0, unroll=4)
+    if split:
+        for x in range(kept_ref.shape[0]):
+            kept_ref[x] = out_ref[0, x]
+            away_ref[x] = out_ref[1, x]
+
+
+def mix(split, upper, place, shifts, weights, quarters, left, right, pair, into):
+    quarter, moments, rows, columns = quarters[0].shape
+    block = (quarter // 2 if split else quarter, moments, rows, columns)
+    shape = block if split else (2 * block[0], *block[1:])
+    outs = 2 if split else 1
+    vmem = pl.BlockSpec(memory_space=pltpu.VMEM)
     smem = pl.BlockSpec(memory_space=pltpu.SMEM)
-    held = [] if into is None else [into]
+    scratch = [pltpu.VMEM((3 * quarter, *quarters[0].shape[1:]), jnp.float32)]
+    if split:
+        scratch.append(pltpu.VMEM((2, *block), jnp.float32))
     return pl.pallas_call(
-        mix_kernel,
+        functools.partial(mix_kernel, split),
         grid=(1,),
         in_specs=[
             smem,
             smem,
-            hbm,
-            hbm,
-            hbm,
-            hbm,
+            smem,
+            vmem,
+            vmem,
+            vmem,
             pl.BlockSpec((None, *left.shape[1:]), lambda i: (pair, 0, 0)),
             pl.BlockSpec((None, *right.shape[1:]), lambda i: (pair, 0, 0, 0, 0)),
-            *(hbm for _ in held),
+            *(pl.BlockSpec(memory_space=pl.ANY) for _ in into),
         ],
-        out_specs=pl.BlockSpec(
-            (2 * quarter, moments, None, rows, columns), lambda i: (0, 0, pair, 0, 0)
-        ),
-        out_shape=jax.ShapeDtypeStruct(shape, jnp.float32),
-        scratch_shapes=[
-            pltpu.VMEM((4 * quarter, *low.shape[1:]), jnp.float32),
-            pltpu.SemaphoreType.DMA((4,)),
-        ],
-        input_output_aliases={8: 0} if held else {},
-        compiler_params=LIMIT,
-        cost_estimate=pl.CostEstimate(flops=5000000000, bytes_accessed=4000000, transcendentals=0),
+        out_specs=[pl.BlockSpec(block, lambda i: (0 if split else upper, 0, 0, 0))] * outs,
+        out_shape=[jax.ShapeDtypeStruct(shape, jnp.float32)] * outs,
+        scratch_shapes=scratch,
+        input_output_aliases={8 + index: index for index in range(len(into))},
+        compiler_params=LIMIT,
+        cost_estimate=pl.CostEstimate(flops=2500000000, bytes_accessed=2000000, transcendentals=0),
         name="mix",
-    )(shifts, weights, below, low, high, above, left, right, *held)
+    )(place, shifts, weights, *quarters, left, right, *into)
+
+
+def sort_kernel(place, kept_low, kept_high, received_low, received_high, *targets):
+    core, first = place[0], place[1]
+    half = kept_low.shape[0]
+    whole = targets[-1]
+    targets = targets[:-1]
+    for side, pieces in enumerate(((kept_low, kept_high), (received_low, received_high))):
+        for x in range(2 * half):
+            whole[side, x] = pieces[x // half][x % half]
+    for step, target in enumerate(targets):
+        where = lax.rem(first + step, 4)
+        for other in range(4):
+            x = jnp.where(core == 0, other, where)
+            moment = jnp.where(core == 0, where, other)
+            target[core, other] = whole[0, x, moment]
+            target[1 - core, other] = whole[1, x, moment]
+
+
+def turn_kernel(place, *refs):
+    sources, targets = refs[:4], refs[4:]
+    for step, target in enumerate(targets):
+        column = lax.rem(place[2] + step, 4)
+        for behind, source in enumerate(sources):
+            for owner in range(2):
+                target[behind, owner] = source[owner, column]
+
+
+def move(kernel, place, arrays, shape, scratch=()):
+    vmem = pl.BlockSpec(memory_space=pltpu.VMEM)
+    return list(
+        pl.pallas_call(
+            kernel,
+            in_specs=[pl.BlockSpec(memory_space=pltpu.SMEM)] + [vmem] * len(arrays),
+            out_specs=[vmem] * 4,
+            out_shape=[jax.ShapeDtypeStruct(shape, jnp.float32)] * 4,
+            scratch_shapes=scratch,
+            compiler_params=LIMIT,
+            cost_estimate=pl.CostEstimate(flops=1000000, bytes_accessed=2000000, transcendentals=0),
+        )(place, *arrays)
+    )
+
+
+def place_kernel(place, held, *rest):
+    sources, (out, sems) = rest[:4], rest[4:]
+    core, first, second = place[0], place[1], place[2]
+    copies = []
+    for step, source in enumerate(sources):
+        along_second = lax.rem(second + 4 - step, 4)
+        for behind in range(4):
+            along_first = lax.rem(first + 4 - behind, 4)
+            x = jnp.where(core == 0, along_second, along_first)
+            y = jnp.where(core == 0, along_first, along_second)
+            for owner in range(2):
+                pair = x * 8 + owner * 4 + y
+                copies.append(
+                    pltpu.make_async_copy(
+                        source.at[behind, owner], out.at[pair, 0], sems.at[step, behind, owner]
+                    )
+                )
+    for copy in copies:
+        copy.start()
+    for copy in copies:
+        copy.wait()
+
+
+def fill_kernel(back, out, sem):
+    copy = pltpu.make_async_copy(back, out.at[:, 1], sem.at[0])
+    copy.start()
+    copy.wait()
+
+
+def put(place, landed, back):
+    group, rows, columns = back.shape
+    hbm = pl.BlockSpec(memory_space=pl.ANY)
+    result = jax.ShapeDtypeStruct((group, 2, rows, columns), jnp.float32)
+    cost = pl.CostEstimate(flops=1000000, bytes_accessed=4000000, transcendentals=0)
+    half = pl.pallas_call(
+        fill_kernel,
+        in_specs=[hbm],
+        out_specs=hbm,
+        out_shape=result,
+        scratch_shapes=[pltpu.SemaphoreType.DMA((1,))],
+        compiler_params=LIMIT,
+        cost_estimate=cost,
+        name="fill",
+    )(back)
+    return pl.pallas_call(
+        place_kernel,
+        in_specs=[pl.BlockSpec(memory_space=pltpu.SMEM)] + [hbm] * 5,
+        out_specs=hbm,
+        out_shape=result,
+        scratch_shapes=[pltpu.SemaphoreType.DMA((4, 4, 2))],
+        input_output_aliases={1: 0},
+        compiler_params=LIMIT,
+        cost_estimate=cost,
+        name="place",
+    )(place, half, *landed)
+
+
+def ring(fn):
+    sizes = [lax.axis_size(axis) for axis in AXES]
+    pairs = []
+    for z, x, c, y in itertools.product(*map(range, sizes)):
+        tx, tc, ty = fn(x, c, y)
+        pairs.append((((z * sizes[1] + x) * sizes[2] + c) * sizes[3] + y,
+                      ((z * sizes[1] + tx % 4) * sizes[2] + tc) * sizes[3] + ty % 4))
+    return pairs
+
+
+def along(step, core):
+    return ring(lambda x, c, y: (x, c, y + step) if c == core else (x + step, c, y))
 
 
 def on_device(green_less, couplings, pair_atoms, shift_idx, weights):
@@ -201,6 +317,10 @@
     down = [(plane + 1, plane) for plane in range(planes - 1)]
     owned = pairs // group
     atoms = lax.dynamic_slice_in_dim(pair_atoms, here * owned, owned, 0)
+    couplings = pltpu.with_memory_space_constraint(couplings, pltpu.HBM)
+    x, c, y = (lax.axis_index(axis) for axis in GROUP)
+    first, second = jnp.where(c == 0, y, x), jnp.where(c == 0, x, y)
+    place = jnp.stack([c, first, second]).astype(jnp.int32)
     left, right = tables(atoms, couplings)
     moved = lax.all_to_all(
         green_less.reshape(group, owned, rows, columns), GROUP, 0, 0, tiled=True
@@ -209,14 +329,34 @@
     halves = []
     for pair in range(owned):
         low, high = fold(block, pair)
-        halves.append((lax.ppermute(high, "z", up), low, high, lax.ppermute(low, "z", down)))
-    result = None
-    for pair in range(owned):
-        result = mix(shift_idx, weights, *halves[pair], left, right, pair, owned, result)
-    back = lax.all_to_all(
-        result.reshape(group, owned, rows, columns), GROUP, 0, 0, tiled=True
-    )
-    return back.reshape(green_less.shape)
+        below = lax.ppermute(high, "z", up)
+        above = lax.ppermute(low, "z", down)
+        halves.append((below, low, high, above))
+
+    def compute(split, upper, pair, into=()):
+        quarters = halves[pair][upper : upper + 3]
+        return mix(split, upper, place, shift_idx, weights, quarters, left, right, pair, into)
+
+    kept, received = [], []
+    for upper in range(2):
+        stay, away = compute(True, upper, 0)
+        received.append(lax.ppermute(away, AXES, ring(lambda x, c, y: (x, 1 - c, y))))
+        kept.append(stay)
+    arrived = move(
+        sort_kernel,
+        place,
+        (*kept, *received),
+        (2, 4, rows, columns),
+        [pltpu.VMEM((2, 4, 4, rows, columns), jnp.float32)],
+    )
+    for step in (2, 1, 3):
+        arrived[step] = lax.ppermute(arrived[step], AXES, along(step, 0))
+    (result,) = compute(False, 1, 1, compute(False, 0, 1))
+    back = lax.all_to_all(result.reshape(group, rows, columns), GROUP, 0, 0, tiled=True)
+    landed = move(turn_kernel, place, arrived, (4, 2, rows, columns))
+    for step in (2, 1, 3):
+        landed[step] = lax.ppermute(landed[step], AXES, along(step, 1))
+    return put(place, landed, back).reshape(green_less.shape)
 
 
 def solution(mesh):
@@ -227,13 +367,10 @@
     )
     placed = P("y", ("z", "x", "c"), None, None, None)
 
-    def step(*args):
-        return jax.shard_map(
-            on_device,
-            mesh=split,
-            in_specs=(placed, P(), P(), P(), P()),
-            out_specs=placed,
-            check_vma=False,
-        )(*args)
-
-    return step
+    return jax.shard_map(
+        on_device,
+        mesh=split,
+        in_specs=(placed, P(), P(), P(), P()),
+        out_specs=placed,
+        check_vma=False,
+    )

time: 107 us -> 110 us (1.028)
  blocking collectives: 68 us -> 35.7 us
  starting transfers between devices: 14 us -> 29.1 us
  waiting for transfers between devices: 10.3 us -> 24.8 us
  Pallas kernels: 10.9 us -> 16.6 us
    all_to_all x1 -> x0, blocking collectives: 32.3 us -> none  [on_device(): lax.all_to_all(result.reshape(group, owned, rows, columns), GROUP, 0, 0,...]
    ppermute x4 -> x12, waiting for transfers between devices: 10.3 us -> 24.8 us  [the longest x3 10.5 us: on_device(): arrived[step] = lax.ppermute(arrived[step], AXES, along(step, 0))]
    ppermute x4 -> x12, starting transfers between devices: 14 us -> 24.9 us  [the longest x2 7.96 us: on_device(): below = lax.ppermute(high, 'z', up)]
    pallas_call x2 -> x8, Pallas kernels: 8.67 us -> 14.8 us  [the longest x4 10.7 us: mix(): pl.pallas_call(functools.partial(mix_kernel, split), grid=(1,), in_specs=...]
    all_to_all x0 -> x1, starting transfers between devices: none -> 4.22 us  [on_device(): lax.all_to_all(result.reshape(group, rows, columns), GROUP, 0, 0, tiled=T...]
    unnamed x11 -> x12, local copies, waits for them, and re-layouts: 2.84 us -> 1.94 us
  transfers between devices with their start and end apart: 4 -> 13, of which waited for: 2 -> 7; matrix products, arithmetic and copies ran while one was open for 0% -> 0% of each run, Pallas kernels for 6% -> 14%
where the time goes in v2:
time: 110 us; the launch traced here: 109 us
  blocking collectives  35.7 us (32%)
  starting transfers between devices  29.1 us (26%)
  waiting for transfers between devices  24.8 us (23%)
  Pallas kernels  16.6 us (15%)
  local copies, waits for them, and re-layouts  2.02 us (2%)
    all_to_all x1, blocking collectives, on_device(): lax.all_to_all(green_less.reshape(group, owned, rows, columns), GROUP, 0,...  35.7 us
    pallas_call x4, Pallas kernels, mix(): pl.pallas_call(functools.partial(mix_kernel, split), grid=(1,), in_specs=...  10.7 us
    ppermute x3, waiting for transfers between devices, on_device(): arrived[step] = lax.ppermute(arrived[step], AXES, along(step, 0))  10.5 us
    ppermute x2, waiting for transfers between devices, on_device(): below = lax.ppermute(high, 'z', up)  8.27 us
    ppermute x2, starting transfers between devices, on_device(): below = lax.ppermute(high, 'z', up)  7.96 us
    ppermute x3, starting transfers between devices, on_device(): arrived[step] = lax.ppermute(arrived[step], AXES, along(step, 0))  6 us
    ppermute x3, starting transfers between devices, on_device(): landed[step] = lax.ppermute(landed[step], AXES, along(step, 1))  5.63 us
    ppermute x2, starting transfers between devices, on_device(): above = lax.ppermute(low, 'z', down)  4.83 us
  transfers between devices with their start and end apart: 13, of which 7 were waited for; matrix products, arithmetic and copies ran while one was open for 0% of the time, Pallas kernels for 14%

profile of v2, /device:TPU:96, one launch (start us, length us, event | category | flops | bytes accessed | tf_op | source)
XLA Modules:
  0.0 108.5 jit_solution(11995455853595707174)
XLA Ops:
  0.0 0.0 copy-start
  0.0 35.7 %all_to_all.10 = f32[32,2,64,128]{3,2,1,0:T(8,128)S(1)} all-to-all(f32[32,2,64,128]{3,2,1,0:T(8,128)} %bitcast.9), channel_id=1, replica_groups=mesh['z'=8,'x'=4,'c'=2,'y'=4] {'x','c','y'}, dimensions={0} | all-to-all | bytes 4194304 | tf_op jit(solution)/shard_map/all_to_all | solution.py:325
  35.7 0.1 fold.3
  35.8 0.0 copy-start.3
  35.8 5.0 %collective-permute-start.2 = (f32[4,4,64,128]{3,2,1,0:T(8,128)S(1)}, f32[4,4,64,128]{3,2,1,0:T(8,128)S(1)}, u32[]{:S(2)}, u32[]{:S(2)}) collective-permute-start(f32[4,4,64,128]{3,2,1,0:T(8,128)S(1)} %get-tuple-element.27.third_ref.second_ref), channel_id=1, source_target_pairs={{0,32},{32,64},{64,96},{96,128},{128,160},{160,192},{192,224},{1,3... | collective-permute-start | bytes 1572872 | tf_op jit(solution)/shard_map/ppermute | solution.py:332
  40.9 0.1 fold.2
  41.0 2.9 %collective-permute-start.1 = (f32[4,4,64,128]{3,2,1,0:T(8,128)S(1)}, f32[4,4,64,128]{3,2,1,0:T(8,128)}, u32[]{:S(2)}, u32[]{:S(2)}) collective-permute-start(f32[4,4,64,128]{3,2,1,0:T(8,128)S(1)} %get-tuple-element.24.third_ref.second_ref), channel_id=1, source_target_pairs={{0,32},{32,64},{64,96},{96,128},{128,160},{160,192},{192,224},{1,3... | collective-permute-start | bytes 1572872 | tf_op jit(solution)/shard_map/ppermute | solution.py:332
  43.9 0.0 copy-done
  43.9 0.1 constant_dynamic-slice_fusion
  44.0 2.9 %collective-permute-start = (f32[4,4,64,128]{3,2,1,0:T(8,128)S(1)}, f32[4,4,64,128]{3,2,1,0:T(8,128)}, u32[]{:S(2)}, u32[]{:S(2)}) collective-permute-start(f32[4,4,64,128]{3,2,1,0:T(8,128)S(1)} %get-tuple-element.23.second_ref.first_ref), channel_id=1, source_target_pairs={{32,0},{64,32},{96,64},{128,96},{160,128},{192,160},{224,192},{33,... | collective-permute-start | bytes 1572872 | tf_op jit(solution)/shard_map/ppermute | solution.py:333
  46.9 0.1 pad_add_fusion.place
  47.0 0.1 copy.13.atoms
  47.1 0.0 copy-done.4
  47.1 1.7 %tables.1 = (bf16[2,64,384]{2,1,0:T(8,128)(2,1)S(1)}, bf16[2,3,2,128,128]{4,3,2,1,0:T(8,128)(2,1)S(1)}) custom-call(s32[2,2]{1,0:T(2,128)S(1)} %copy.13.atoms, bf16[32,3,64,64]{3,2,1,0:T(8,128)(2,1)} %coupling_hbm.1), custom_call_target="tpu_custom_call" | custom-call | flops 1000000 | bytes 4000000 | tf_op jit(solution)/shard_map/tables/pallas_call | solution.py:49
  48.8 1.9 %collective-permute-start.3 = (f32[4,4,64,128]{3,2,1,0:T(8,128)S(1)}, f32[4,4,64,128]{3,2,1,0:T(8,128)}, u32[]{:S(2)}, u32[]{:S(2)}) collective-permute-start(f32[4,4,64,128]{3,2,1,0:T(8,128)S(1)} %get-tuple-element.28.second_ref.first_ref), channel_id=1, source_target_pairs={{32,0},{64,32},{96,64},{128,96},{160,128},{192,160},{224,192},{33,... | collective-permute-start | bytes 1572872 | tf_op jit(solution)/shard_map/ppermute | solution.py:333
  50.7 2.4 %collective-permute-done.2.first_ref = f32[4,4,64,128]{3,2,1,0:T(8,128)S(1)} collective-permute-done((f32[4,4,64,128]{3,2,1,0:T(8,128)S(1)}, f32[4,4,64,128]{3,2,1,0:T(8,128)S(1)}, u32[]{:S(2)}, u32[]{:S(2)}) %collective-permute-start.2) | collective-permute-done | bytes 524320 | tf_op jit(solution)/shard_map/ppermute | solution.py:332
  53.2 0.8 copy-done.1
  54.0 0.0 copy-done.3
  54.0 1.0 copy-done.2
  55.0 2.0 %mix.6 = (f32[2,4,64,128]{3,2,1,0:T(8,128)S(1)}, f32[2,4,64,128]{3,2,1,0:T(8,128)S(1)}) custom-call(s32[3]{0:T(128)S(1)} %pad_add_fusion.place, s32[3]{0:T(128)S(1)} %copy-done.3, f32[2,3,4]{2,1,0:T(4,128)S(1)} %copy.10.weights, f32[4,4,64,128]{3,2,1,0:T(8,128)S(1)} %copy-done.2, f32[4,4,64,128]{3,2,1,0:T(8,128)S(1)} %get-tuple-element.28.second_ref.first_ref, ...), custom_call_target="tpu_custom_call" | custom-call | flops 2500000000 | bytes 2000000 | tf_op jit(solution)/shard_map/mix/pallas_call | solution.py:174
  57.0 0.1 collective-permute-start.4
  57.1 5.8 %collective-permute-done.1.first_ref = f32[4,4,64,128]{3,2,1,0:T(8,128)} collective-permute-done((f32[4,4,64,128]{3,2,1,0:T(8,128)S(1)}, f32[4,4,64,128]{3,2,1,0:T(8,128)}, u32[]{:S(2)}, u32[]{:S(2)}) %collective-permute-start.1) | collective-permute-done | bytes 524320 | tf_op jit(solution)/shard_map/ppermute | solution.py:332
  62.9 3.2 %mix.4.rest_0_ = f32[8,4,64,128]{3,2,1,0:T(8,128)} custom-call(s32[3]{0:T(128)S(1)} %pad_add_fusion.place, s32[3]{0:T(128)S(1)} %copy-done.3, f32[2,3,4]{2,1,0:T(4,128)S(1)} %copy.10.weights, f32[4,4,64,128]{3,2,1,0:T(8,128)} %collective-permute-done.1.first_ref, f32[4,4,64,128]{3,2,1,0:T(8,128)S(1)} %get-tuple-element.23.second_ref.first_ref, ...), custom_call_target="tpu_custom_call" | custom-call | flops 2500000000 | bytes 2000000 | tf_op jit(solution)/shard_map/mix/pallas_call | solution.py:174
  66.1 0.0 collective-permute-done.third_ref
  66.1 3.2 %mix.5 = f32[8,4,64,128]{3,2,1,0:T(8,128)} custom-call(s32[3]{0:T(128)S(1)} %pad_add_fusion.place, s32[3]{0:T(128)S(1)} %copy-done.3, f32[2,3,4]{2,1,0:T(4,128)S(1)} %copy.10.weights, f32[4,4,64,128]{3,2,1,0:T(8,128)S(1)} %get-tuple-element.23.second_ref.first_ref, ...), custom_call_target="tpu_custom_call", output_to_operand_aliasing={{}: (8, {})} | custom-call | flops 2500000000 | bytes 2000000 | tf_op jit(solution)/shard_map/mix/pallas_call | solution.py:174
  69.2 4.2 %all-to-all-start.1 = ((f32[32,64,128]{2,1,0:T(8,128)}), f32[32,64,128]{2,1,0:T(8,128)S(1)}, u32[]{:S(2)}, u32[]{:S(2)}) async-start(f32[32,64,128]{2,1,0:T(8,128)} %bitcast.5), calls=%async_computation.1 | async-start | bytes 2097152 | tf_op jit(solution)/shard_map/all_to_all | solution.py:355
  73.5 0.0 collective-permute-done.3.third_ref
  73.5 2.4 %mix.7 = (f32[2,4,64,128]{3,2,1,0:T(8,128)S(1)}, f32[2,4,64,128]{3,2,1,0:T(8,128)S(1)}) custom-call(s32[3]{0:T(128)S(1)} %pad_add_fusion.place, s32[3]{0:T(128)S(1)} %copy-done.3, f32[2,3,4]{2,1,0:T(4,128)S(1)} %copy.10.weights, f32[4,4,64,128]{3,2,1,0:T(8,128)S(1)} %get-tuple-element.28.second_ref.first_ref, ...), custom_call_target="tpu_custom_call" | custom-call | flops 2500000000 | bytes 2000000 | tf_op jit(solution)/shard_map/mix/pallas_call | solution.py:174
  75.9 0.4 collective-permute-start.5
  76.3 0.0 collective-permute-done.4.received_low
  76.3 1.3 %collective-permute-done.5.received_high = f32[2,4,64,128]{3,2,1,0:T(8,128)S(1)} collective-permute-done((f32[2,4,64,128]{3,2,1,0:T(8,128)S(1)}, f32[2,4,64,128]{3,2,1,0:T(8,128)S(1)}, u32[]{:S(2)}, u32[]{:S(2)}) %collective-permute-start.5) | collective-permute-done | bytes 262176 | tf_op jit(solution)/shard_map/ppermute | solution.py:343
  77.5 0.7 shard_map.55
  78.2 1.9 %collective-permute-start.6 = (f32[2,4,64,128]{3,2,1,0:T(8,128)S(1)}, f32[2,4,64,128]{3,2,1,0:T(8,128)S(1)}, u32[]{:S(2)}, u32[]{:S(2)}) collective-permute-start(f32[2,4,64,128]{3,2,1,0:T(8,128)S(1)} %get-tuple-element.34), channel_id=1, source_target_pairs={{0,1},{1,2},{2,3},{3,0},{4,12},{5,13},{6,14},{7,15},{8,9},{9,10},{... | collective-permute-start | bytes 786440 | tf_op jit(solution)/shard_map/ppermute | solution.py:353
  80.1 2.7 %collective-permute-start.7 = (f32[2,4,64,128]{3,2,1,0:T(8,128)S(1)}, f32[2,4,64,128]{3,2,1,0:T(8,128)S(1)}, u32[]{:S(2)}, u32[]{:S(2)}) collective-permute-start(f32[2,4,64,128]{3,2,1,0:T(8,128)S(1)} %get-tuple-element.35), channel_id=1, source_target_pairs={{0,2},{1,3},{2,0},{3,1},{4,20},{5,21},{6,22},{7,23},{8,10},{9,11},... | collective-permute-start | bytes 786440 | tf_op jit(solution)/shard_map/ppermute | solution.py:353
  82.8 1.5 %collective-permute-start.8 = (f32[2,4,64,128]{3,2,1,0:T(8,128)S(1)}, f32[2,4,64,128]{3,2,1,0:T(8,128)S(1)}, u32[]{:S(2)}, u32[]{:S(2)}) collective-permute-start(f32[2,4,64,128]{3,2,1,0:T(8,128)S(1)} %get-tuple-element.36), channel_id=1, source_target_pairs={{0,3},{1,0},{2,1},{3,2},{4,28},{5,29},{6,30},{7,31},{8,11},{9,8},{... | collective-permute-start | bytes 786440 | tf_op jit(solution)/shard_map/ppermute | solution.py:353
  84.2 7.7 %collective-permute-done.6.refs_1_ = f32[2,4,64,128]{3,2,1,0:T(8,128)S(1)} collective-permute-done((f32[2,4,64,128]{3,2,1,0:T(8,128)S(1)}, f32[2,4,64,128]{3,2,1,0:T(8,128)S(1)}, u32[]{:S(2)}, u32[]{:S(2)}) %collective-permute-start.6) | collective-permute-done | bytes 262176 | tf_op jit(solution)/shard_map/ppermute | solution.py:353
  91.9 2.9 %collective-permute-done.7.refs_2_ = f32[2,4,64,128]{3,2,1,0:T(8,128)S(1)} collective-permute-done((f32[2,4,64,128]{3,2,1,0:T(8,128)S(1)}, f32[2,4,64,128]{3,2,1,0:T(8,128)S(1)}, u32[]{:S(2)}, u32[]{:S(2)}) %collective-permute-start.7) | collective-permute-done | bytes 262176 | tf_op jit(solution)/shard_map/ppermute | solution.py:353
  94.8 0.0 collective-permute-done.8.refs_3_
  94.8 0.6 shard_map.56
  95.4 1.6 %collective-permute-start.9 = (f32[4,2,64,128]{3,2,1,0:T(8,128)S(1)}, f32[4,2,64,128]{3,2,1,0:T(8,128)S(1)}, u32[]{:S(2)}, u32[]{:S(2)}) collective-permute-start(f32[4,2,64,128]{3,2,1,0:T(8,128)S(1)} %get-tuple-element.38), channel_id=1, source_target_pairs={{0,8},{1,9},{2,10},{3,11},{4,5},{5,6},{6,7},{7,4},{8,16},{9,17},{1... | collective-permute-start | bytes 786440 | tf_op jit(solution)/shard_map/ppermute | solution.py:358
  96.9 2.7 %collective-permute-start.10 = (f32[4,2,64,128]{3,2,1,0:T(8,128)S(1)}, f32[4,2,64,128]{3,2,1,0:T(8,128)S(1)}, u32[]{:S(2)}, u32[]{:S(2)}) collective-permute-start(f32[4,2,64,128]{3,2,1,0:T(8,128)S(1)} %get-tuple-element.39), channel_id=1, source_target_pairs={{0,16},{1,17},{2,18},{3,19},{4,6},{5,7},{6,4},{7,5},{8,24},{9,25},... | collective-permute-start | bytes 786440 | tf_op jit(solution)/shard_map/ppermute | solution.py:358
  99.6 1.4 %collective-permute-start.11 = (f32[4,2,64,128]{3,2,1,0:T(8,128)S(1)}, f32[4,2,64,128]{3,2,1,0:T(8,128)S(1)}, u32[]{:S(2)}, u32[]{:S(2)}) collective-permute-start(f32[4,2,64,128]{3,2,1,0:T(8,128)S(1)} %get-tuple-element.40), channel_id=1, source_target_pairs={{0,24},{1,25},{2,26},{3,27},{4,7},{5,4},{6,5},{7,6},{8,0},{9,1},{1... | collective-permute-start | bytes 786440 | tf_op jit(solution)/shard_map/ppermute | solution.py:358
  101.0 0.0 all-to-all-done.1.back
  101.0 1.0 fill.1.held
  102.0 1.0 collective-permute-done.9.rest_1_
  103.0 3.7 %collective-permute-done.10.rest_2_ = f32[4,2,64,128]{3,2,1,0:T(8,128)S(1)} collective-permute-done((f32[4,2,64,128]{3,2,1,0:T(8,128)S(1)}, f32[4,2,64,128]{3,2,1,0:T(8,128)S(1)}, u32[]{:S(2)}, u32[]{:S(2)}) %collective-permute-start.10) | collective-permute-done | bytes 262176 | tf_op jit(solution)/shard_map/ppermute | solution.py:358
  106.8 0.0 collective-permute-done.11.rest_3_
  106.8 1.8 %place.1 = f32[32,2,64,128]{3,2,1,0:T(8,128)} custom-call(s32[3]{0:T(128)S(1)} %pad_add_fusion.place, f32[32,2,64,128]{3,2,1,0:T(8,128)} %fill.1.held, f32[4,2,64,128]{3,2,1,0:T(8,128)S(1)} %get-tuple-element.37.rest_0_, f32[4,2,64,128]{3,2,1,0:T(8,128)S(1)} %collective-permute-done.9.rest_1_, ...), custom_call_target="tpu_custom_call", output_to_operand_aliasing={{}: (1, {})} | custom-call | flops 1000000 | bytes 4000000 | tf_op jit(solution)/shard_map/place/pallas_call | solution.py:283
  (4 shorter events, 0.0 us)
Async XLA Ops:
  0.0 43.9 %copy-start = (s32[64,2]{0,1:T(2,128)S(1)}, s32[64,2]{0,1:T(2,128)}, u32[]{:S(2)}) copy-start(s32[64,2]{0,1:T(2,128)} %param.7) | copy-start | bytes 1540
  35.7 11.3 %copy-start.4 = (f32[2,3,4]{2,0,1:T(2,128)S(1)}, f32[2,3,4]{2,0,1:T(2,128)}, u32[]{:S(2)}) copy-start(f32[2,3,4]{2,0,1:T(2,128)} %param.9) | copy-start | bytes 292
  35.8 18.1 %copy-start.3 = (s32[3]{0:T(128)S(1)}, s32[3]{0:T(128)}, u32[]{:S(2)}) copy-start(s32[3]{0:T(128)} %shifts.7) | copy-start | bytes 40
  35.8 17.3 %collective-permute-start.2 = (f32[4,4,64,128]{3,2,1,0:T(8,128)S(1)}, f32[4,4,64,128]{3,2,1,0:T(8,128)S(1)}, u32[]{:S(2)}, u32[]{:S(2)}) collective-permute-start(f32[4,4,64,128]{3,2,1,0:T(8,128)S(1)} %get-tuple-element.27.third_ref.second_ref), channel_id=1, source_target_pairs={{0,32},{32,64},{64,96},{96,128},{128,160},{160,192},{192,224},{1,3... | collective-permute-start | bytes 1572872 | tf_op jit(solution)/shard_map/ppermute | solution.py:332
  41.0 21.9 %collective-permute-start.1 = (f32[4,4,64,128]{3,2,1,0:T(8,128)S(1)}, f32[4,4,64,128]{3,2,1,0:T(8,128)}, u32[]{:S(2)}, u32[]{:S(2)}) collective-permute-start(f32[4,4,64,128]{3,2,1,0:T(8,128)S(1)} %get-tuple-element.24.third_ref.second_ref), channel_id=1, source_target_pairs={{0,32},{32,64},{64,96},{96,128},{128,160},{160,192},{192,224},{1,3... | collective-permute-start | bytes 1572872 | tf_op jit(solution)/shard_map/ppermute | solution.py:332
  44.0 22.1 %collective-permute-start = (f32[4,4,64,128]{3,2,1,0:T(8,128)S(1)}, f32[4,4,64,128]{3,2,1,0:T(8,128)}, u32[]{:S(2)}, u32[]{:S(2)}) collective-permute-start(f32[4,4,64,128]{3,2,1,0:T(8,128)S(1)} %get-tuple-element.23.second_ref.first_ref), channel_id=1, source_target_pairs={{32,0},{64,32},{96,64},{128,96},{160,128},{192,160},{224,192},{33,... | collective-permute-start | bytes 1572872 | tf_op jit(solution)/shard_map/ppermute | solution.py:333
  48.8 24.7 %collective-permute-start.3 = (f32[4,4,64,128]{3,2,1,0:T(8,128)S(1)}, f32[4,4,64,128]{3,2,1,0:T(8,128)}, u32[]{:S(2)}, u32[]{:S(2)}) collective-permute-start(f32[4,4,64,128]{3,2,1,0:T(8,128)S(1)} %get-tuple-element.28.second_ref.first_ref), channel_id=1, source_target_pairs={{32,0},{64,32},{96,64},{128,96},{160,128},{192,160},{224,192},{33,... | collective-permute-start | bytes 1572872 | tf_op jit(solution)/shard_map/ppermute | solution.py:333
  53.2 0.8 copy-start.1
  54.0 1.0 copy-start.2
  57.0 19.3 %collective-permute-start.4 = (f32[2,4,64,128]{3,2,1,0:T(8,128)S(1)}, f32[2,4,64,128]{3,2,1,0:T(8,128)S(1)}, u32[]{:S(2)}, u32[]{:S(2)}) collective-permute-start(f32[2,4,64,128]{3,2,1,0:T(8,128)S(1)} %get-tuple-element.31), channel_id=1, source_target_pairs={{0,4},{1,5},{2,6},{3,7},{4,0},{5,1},{6,2},{7,3},{8,12},{9,13},{10,... | collective-permute-start | bytes 786440 | tf_op jit(solution)/shard_map/ppermute | solution.py:343
  69.2 31.8 %all-to-all-start.1 = ((f32[32,64,128]{2,1,0:T(8,128)}), f32[32,64,128]{2,1,0:T(8,128)S(1)}, u32[]{:S(2)}, u32[]{:S(2)}) async-start(f32[32,64,128]{2,1,0:T(8,128)} %bitcast.5), calls=%async_computation.1 | async-start | bytes 2097152 | tf_op jit(solution)/shard_map/all_to_all | solution.py:355
  75.9 1.6 %collective-permute-start.5 = (f32[2,4,64,128]{3,2,1,0:T(8,128)S(1)}, f32[2,4,64,128]{3,2,1,0:T(8,128)S(1)}, u32[]{:S(2)}, u32[]{:S(2)}) collective-permute-start(f32[2,4,64,128]{3,2,1,0:T(8,128)S(1)} %get-tuple-element.32), channel_id=1, source_target_pairs={{0,4},{1,5},{2,6},{3,7},{4,0},{5,1},{6,2},{7,3},{8,12},{9,13},{10,... | collective-permute-start | bytes 786440 | tf_op jit(solution)/shard_map/ppermute | solution.py:343
  78.2 13.7 %collective-permute-start.6 = (f32[2,4,64,128]{3,2,1,0:T(8,128)S(1)}, f32[2,4,64,128]{3,2,1,0:T(8,128)S(1)}, u32[]{:S(2)}, u32[]{:S(2)}) collective-permute-start(f32[2,4,64,128]{3,2,1,0:T(8,128)S(1)} %get-tuple-element.34), channel_id=1, source_target_pairs={{0,1},{1,2},{2,3},{3,0},{4,12},{5,13},{6,14},{7,15},{8,9},{9,10},{... | collective-permute-start | bytes 786440 | tf_op jit(solution)/shard_map/ppermute | solution.py:353
  80.1 14.7 %collective-permute-start.7 = (f32[2,4,64,128]{3,2,1,0:T(8,128)S(1)}, f32[2,4,64,128]{3,2,1,0:T(8,128)S(1)}, u32[]{:S(2)}, u32[]{:S(2)}) collective-permute-start(f32[2,4,64,128]{3,2,1,0:T(8,128)S(1)} %get-tuple-element.35), channel_id=1, source_target_pairs={{0,2},{1,3},{2,0},{3,1},{4,20},{5,21},{6,22},{7,23},{8,10},{9,11},... | collective-permute-start | bytes 786440 | tf_op jit(solution)/shard_map/ppermute | solution.py:353
  82.8 12.0 %collective-permute-start.8 = (f32[2,4,64,128]{3,2,1,0:T(8,128)S(1)}, f32[2,4,64,128]{3,2,1,0:T(8,128)S(1)}, u32[]{:S(2)}, u32[]{:S(2)}) collective-permute-start(f32[2,4,64,128]{3,2,1,0:T(8,128)S(1)} %get-tuple-element.36), channel_id=1, source_target_pairs={{0,3},{1,0},{2,1},{3,2},{4,28},{5,29},{6,30},{7,31},{8,11},{9,8},{... | collective-permute-start | bytes 786440 | tf_op jit(solution)/shard_map/ppermute | solution.py:353
  95.4 7.7 %collective-permute-start.9 = (f32[4,2,64,128]{3,2,1,0:T(8,128)S(1)}, f32[4,2,64,128]{3,2,1,0:T(8,128)S(1)}, u32[]{:S(2)}, u32[]{:S(2)}) collective-permute-start(f32[4,2,64,128]{3,2,1,0:T(8,128)S(1)} %get-tuple-element.38), channel_id=1, source_target_pairs={{0,8},{1,9},{2,10},{3,11},{4,5},{5,6},{6,7},{7,4},{8,16},{9,17},{1... | collective-permute-start | bytes 786440 | tf_op jit(solution)/shard_map/ppermute | solution.py:358
  96.9 9.8 %collective-permute-start.10 = (f32[4,2,64,128]{3,2,1,0:T(8,128)S(1)}, f32[4,2,64,128]{3,2,1,0:T(8,128)S(1)}, u32[]{:S(2)}, u32[]{:S(2)}) collective-permute-start(f32[4,2,64,128]{3,2,1,0:T(8,128)S(1)} %get-tuple-element.39), channel_id=1, source_target_pairs={{0,16},{1,17},{2,18},{3,19},{4,6},{5,7},{6,4},{7,5},{8,24},{9,25},... | collective-permute-start | bytes 786440 | tf_op jit(solution)/shard_map/ppermute | solution.py:358
  99.6 7.2 %collective-permute-start.11 = (f32[4,2,64,128]{3,2,1,0:T(8,128)S(1)}, f32[4,2,64,128]{3,2,1,0:T(8,128)S(1)}, u32[]{:S(2)}, u32[]{:S(2)}) collective-permute-start(f32[4,2,64,128]{3,2,1,0:T(8,128)S(1)} %get-tuple-element.40), channel_id=1, source_target_pairs={{0,24},{1,25},{2,26},{3,27},{4,7},{5,4},{6,5},{7,6},{8,0},{9,1},{1... | collective-permute-start | bytes 786440 | tf_op jit(solution)/shard_map/ppermute | solution.py:358
